TPU v7x, 32 devices: a whole 2x2x4 slice. The times are simulated.
32 devices in a mesh: ctx: 4 (over y, x), head: 4 (over z), fsdp: 2 (over core).
Axes of the slice: x: 2, y: 2, z: 4, core: 2. Of those that a mesh axis runs over, the one named last changes fastest.
Arguments:
- layer_input: bfloat16 [4096, 4096], P(('ctx', 'fsdp')), may hold values from -6 to 6
- query_act: bfloat16 [4096, 4096], P(('ctx', 'fsdp'), 'head'), may hold values from -6 to 6
- key_act: bfloat16 [4096, 4096], P(('ctx', 'fsdp'), 'head'), may hold values from -6 to 6
- out_grad: bfloat16 [4096, 4096], P(('ctx', 'fsdp'), 'head'), may hold values from -6 to 6
- value_weight: bfloat16 [4096, 4096], P('fsdp', 'head'), may hold values from -0.09375 to 0.09375
Outputs:
- query_grad: bfloat16 [4096, 4096], P(('ctx', 'fsdp'), 'head')
- key_grad: bfloat16 [4096, 4096], P(('ctx', 'fsdp'), 'head')
- input_grad: bfloat16 [4096, 4096], P(('ctx', 'fsdp'), 'head')
- weight_grad: float32 [4096, 4096], P(('ctx', 'fsdp'), 'head')
All inputs are finite; a program needn't handle non-finite values.
Results may differ from a plain program's by a relative error of at most 0.018.
Values may be sent and summed in bfloat16 or wider, within the bound.
A program may use at most 128 MiB of HBM per device.

v0:
```python
import math
import jax
import jax.numpy as jnp
from jax import lax
from jax.sharding import PartitionSpec as P

HDIM = 128


def entering(array, axis, join, neutral):
    place = lax.axis_index(axis)
    gathered = lax.all_gather(array.astype(jnp.bfloat16), axis)
    state = jnp.zeros_like(array) + jnp.asarray(neutral, array.dtype)

    def one(step, state):
        return join(state, lax.dynamic_index_in_dim(gathered, step, 0, False).astype(array.dtype))

    return lax.fori_loop(0, place, one, state)


def as_sent(array):
    return jax.tree.map(lambda a: a.astype(jnp.bfloat16) if a.dtype == jnp.float32 else a, array)


def product(pattern, former, latter):
    return jnp.einsum(pattern, former, latter, precision=lax.Precision.HIGHEST)


def lowdot(pattern, former, latter):
    return jnp.einsum(pattern, former, latter, preferred_element_type=jnp.float32)


def add_states(earlier, following):
    return earlier + following


def norm_grad(attended, grad_heads):
    inverse_rms = lax.rsqrt(jnp.mean(attended * attended, axis=-1, keepdims=True) + 1e-05)
    normed = attended * inverse_rms
    return inverse_rms * (
        grad_heads - normed * jnp.mean(grad_heads * normed, axis=-1, keepdims=True)
    )


def local(layer_input, query_act, key_act, out_grad, value_weight):
    tok_rows = layer_input.shape[0]
    weight_full = lax.all_gather(value_weight, "fsdp", axis=0, tiled=True)
    value_act = jnp.dot(layer_input, weight_full, preferred_element_type=jnp.float32).astype(
        jnp.bfloat16
    )
    heads_dev = query_act.shape[1] // HDIM
    head_shape = (tok_rows, heads_dev, HDIM)
    query_heads = query_act.reshape(head_shape)
    key_heads = key_act.reshape(head_shape)
    value_heads = value_act.reshape(head_shape)
    query_wide = query_heads.astype(jnp.float32)
    key_wide = key_heads.astype(jnp.float32)
    value_wide = value_heads.astype(jnp.float32)
    grad_wide = out_grad.reshape(head_shape).astype(jnp.float32)
    pair_sum = lowdot("shi,shj->hij", key_heads, value_heads)
    state_prev = entering(pair_sum, ("ctx", "fsdp"), add_states, jnp.zeros_like(pair_sum))
    causal = jnp.tril(jnp.ones((tok_rows, tok_rows), dtype=bool))
    scores = lowdot("thi,shi->hts", query_heads, key_heads)
    masked = jnp.where(causal[None], scores, 0.0).astype(jnp.bfloat16)
    attended = lowdot("hts,shj->thj", masked, value_heads) + product(
        "thi,hij->thj", query_wide, state_prev
    )
    attn_grad = norm_grad(attended, grad_wide)
    attn_low = attn_grad.astype(jnp.bfloat16)
    local_grad = product("thi,thj->hij", query_wide, attn_grad)
    own_index = lax.axis_index(("ctx", "fsdp"))
    gathered = lax.all_gather(as_sent(local_grad[None]), ("ctx", "fsdp"), axis=0, tiled=True)
    owners = jnp.arange(gathered.shape[0], dtype=jnp.int32)
    is_later = (owners > own_index)[:, None, None, None]
    state_grad = jnp.zeros_like(local_grad) + jnp.sum(jnp.where(is_later, gathered, 0.0), axis=0)
    cross_terms = jnp.where(
        causal[None], lowdot("thj,shj->hts", attn_low, value_heads), 0.0
    ).astype(jnp.bfloat16)
    query_part = lowdot("hts,shi->thi", cross_terms, key_heads) + product(
        "hij,thj->thi", state_prev, attn_grad
    )
    key_part = lowdot("hts,thi->shi", cross_terms, query_heads) + product(
        "hij,shj->shi", state_grad, value_wide
    )
    value_part = lowdot("hts,thj->shj", masked, attn_low) + product(
        "shi,hij->shj", key_wide, state_grad
    )
    query_grad = query_part.reshape(tok_rows, -1).astype(jnp.bfloat16)
    key_grad = key_part.reshape(tok_rows, -1).astype(jnp.bfloat16)
    value_grad = value_part.reshape(tok_rows, -1).astype(jnp.bfloat16)
    seq_devices = lax.axis_size(("ctx", "fsdp"))
    grad_scale = 1.0 / math.sqrt(tok_rows * seq_devices)
    weight_grad = lax.psum_scatter(
        (
            lax.dot_general(
                layer_input,
                value_grad,
                (((0,), (0,)), ((), ())),
                preferred_element_type=jnp.float32,
            )
            * grad_scale
        ).astype(jnp.bfloat16),
        ("ctx", "fsdp"),
        scatter_dimension=0,
        tiled=True,
    ).astype(jnp.float32)
    partial_input = lax.dot_general(
        value_grad, weight_full, (((1,), (1,)), ((), ())), preferred_element_type=jnp.float32
    )
    input_grad = lax.psum_scatter(
        partial_input.astype(jnp.bfloat16), "head", scatter_dimension=1, tiled=True
    )
    return (query_grad, key_grad, input_grad, weight_grad)


def solution(mesh):
    in_specs = (
        P(("ctx", "fsdp"), None),
        P(("ctx", "fsdp"), "head"),
        P(("ctx", "fsdp"), "head"),
        P(("ctx", "fsdp"), "head"),
        P("fsdp", "head"),
    )
    out_specs = (
        P(("ctx", "fsdp"), "head"),
        P(("ctx", "fsdp"), "head"),
        P(("ctx", "fsdp"), "head"),
        P(("ctx", "fsdp"), "head"),
    )
    return jax.shard_map(local, mesh=mesh, in_specs=in_specs, out_specs=out_specs, check_vma=False)
```

profile of v0, /device:TPU:0, one launch (start us, length us, event | category | flops | bytes accessed | tf_op | source)
XLA Modules:
  0.0 283.1 jit_solution(3473864413043663214)
XLA Ops:
  8.0 24.2 %all-gather.6.cloned.1.call-done = bf16[4096,1024]{1,0:T(8,128)(2,1)} async-done(((bf16[2048,1024]{1,0:T(8,128)(2,1)}), bf16[4096,1024]{1,0:T(8,128)(2,1)}) %all-gather.6.cloned.1.call-update) | async-done | bytes 8388624 | tf_op jit(solution)/shard_map/all_gather | solution.py:47
  32.1 9.1 %fusion.2 = bf16[64,8,8,128]{3,2,1,0:T(8,128)(2,1)S(1)} fusion(bf16[512,4096]{1,0:T(8,128)(2,1)} %param.7, bf16[4096,1024]{1,0:T(8,128)(2,1)} %all-gather.6.cloned.1.call-done), kind=kOutput, calls=%fused_computation.17 | convolution fusion | flops 4295491584 | bytes 13631488 | tf_op jit(solution)/shard_map/dot_general | solution.py:48
  42.8 2.6 copy.60
  45.5 1.3 select_convert_fusion.1
  46.8 2.0 copy-done.5
  48.8 2.9 %fusion.16 = f32[8,128,512]{2,1,0:T(8,128)} fusion(bf16[8,512,512]{2,1,0:T(8,128)(2,1)S(1)} %select_convert_fusion.1, bf16[64,8,8,128]{3,2,1,0:T(8,128)(2,1)S(1)} %fusion.2), kind=kOutput, calls=%fused_computation.33 | convolution fusion | flops 536870912 | bytes 7340032 | tf_op jit(solution)/shard_map/hts,shj->thj/dot_general | solution.py:30
  51.6 20.2 %all-gather.8.cloned.1.call-done = bf16[64,128,128]{2,1,0:T(8,128)(2,1)} async-done(((bf16[8,128,128]{2,1,0:T(8,128)(2,1)}), bf16[64,128,128]{2,1,0:T(8,128)(2,1)}) %all-gather.8.cloned.1.call-update) | async-done | bytes 2097168 | tf_op jit(solution)/shard_map/all_gather | solution.py:12
  71.9 3.0 %fusion.1 = (f32[512,8]{0,1:T(8,128)S(1)}, f32[8,128,512]{2,1,0:T(8,128)S(1)}) fusion(f32[8,128,512]{2,1,0:T(8,128)} %fusion.16, f32[8,128,128]{2,1,0:T(8,128)S(1)} %get-tuple-element.27, bf16[512,1024]{1,0:T(8,128)(2,1)S(1)} %copy-done), kind=kOutput, calls=%fused_computation.8 | convolution fusion | flops 806875136 | bytes 5783552 | tf_op jit(solution)/shard_map/thi,hij->thj/dot_general | solution.py:26
  76.1 1.2 fusion.3
  78.4 4.2 %fusion.32 = f32[8,128,512]{2,1,0:T(8,128)} fusion(bf16[8,512,512]{2,1,0:T(8,128)(2,1)} %copy-done.5, f32[512,8,128]{0,2,1:T(8,128)S(1)} %subtract_multiply_fusion), kind=kOutput, calls=%fused_computation.50 | convolution fusion | flops 537395200 | bytes 8388608 | tf_op jit(solution)/shard_map/hts,thj->shj/dot_general | solution.py:30
  82.6 31.0 %all-gather.10.cloned.1.call-done = bf16[64,128,128]{2,1,0:T(8,128)(2,1)} async-done(((bf16[8,128,128]{2,1,0:T(8,128)(2,1)}), bf16[64,128,128]{2,1,0:T(8,128)(2,1)}) %all-gather.10.cloned.1.call-update) | async-done | bytes 2097168 | tf_op jit(solution)/shard_map/all_gather | solution.py:72
  113.6 2.2 select_reduce_fusion
  115.9 1.9 add_convert_fusion
  118.7 6.8 %fusion = bf16[4096,1024]{0,1:T(8,128)(2,1)} fusion(bf16[512,1024]{0,1:T(8,128)(2,1)S(1)} %bitcast.110, bf16[512,4096]{1,0:T(8,128)(2,1)S(1)} %copy-done.13), kind=kOutput, calls=%fused_computation.4 | convolution fusion | flops 4303355904 | bytes 13631488 | tf_op jit(solution)/shard_map/dot_general | solution.py:95
  125.6 10.6 %convolution_convert_fusion = bf16[512,4096]{1,0:T(8,128)(2,1)} fusion(bf16[512,1024]{0,1:T(8,128)(2,1)} %bitcast.111, bf16[4096,1024]{1,0:T(8,128)(2,1)} %all-gather.6.cloned.1.call-done), kind=kOutput, calls=%fused_computation.5 | convolution fusion | flops 4297064448 | bytes 13631488 | tf_op jit(solution)/shard_map/dot_general | solution.py:107
  136.2 3.0 %select_convert_fusion = bf16[8,512,512]{2,1,0:T(8,128)(2,1)S(1)} fusion(pred[512,512]{1,0:T(8,128)(4,1)} %copy-done.12, bf16[64,8,8,128]{3,2,1,0:T(8,128)(2,1)} %copy-done.6, f32[512,8,128]{0,2,1:T(8,128)S(1)} %subtract_multiply_fusion), kind=kOutput, calls=%fused_computation.2 | convolution fusion | flops 541589504 | bytes 7602176 | tf_op jit(solution)/shard_map/thj,shj->hts/dot_general | solution.py:30
  139.2 1.5 fusion.5
  141.2 3.0 %add_convert_fusion.2 = bf16[8,512,128]{1,2,0:T(8,128)(2,1)} fusion(f32[8,512,128]{1,2,0:T(8,128)S(1)} %fusion.5, f32[512,8,128]{0,2,1:T(8,128)S(1)} %subtract_multiply_fusion, f32[8,128,128]{2,1,0:T(8,128)S(1)} %copy-done.3), kind=kOutput, calls=%fused_computation.12 | convolution fusion | flops 806354944 | bytes 5767168 | tf_op jit(solution)/shard_map/hij,thj->thi/dot_general | solution.py:26
  144.3 2.3 copy.71
  146.5 3.1 %fusion.10 = f32[8,512,128]{1,2,0:T(8,128)S(1)} fusion(bf16[8,512,512]{2,1,0:T(8,128)(2,1)} %copy-done.1, bf16[512,1024]{1,0:T(8,128)(2,1)S(1)} %copy-done), kind=kOutput, calls=%fused_computation.27 | convolution fusion | flops 536870912 | bytes 7340032 | tf_op jit(solution)/shard_map/hts,thi->shi/dot_general | solution.py:30
  150.1 1.3 copy.72
  151.4 45.6 %reduce-scatter.5.cloned.1.call-done = bf16[512,1024]{0,1:T(8,128)(2,1)} async-done(((bf16[4096,1024]{0,1:T(8,128)(2,1)}), bf16[512,1024]{0,1:T(8,128)(2,1)}) %reduce-scatter.5.cloned.1.call-update) | async-done | bytes 1048592 | tf_op jit(solution)/shard_map/reduce_scatter | solution.py:93
  197.0 2.6 copy.73
  199.5 77.0 %reduce-scatter.3.cloned.1.call-done = bf16[512,1024]{1,0:T(8,128)(2,1)} async-done(((bf16[512,4096]{1,0:T(8,128)(2,1)}), bf16[512,1024]{1,0:T(8,128)(2,1)}) %reduce-scatter.3.cloned.1.call-update) | async-done | bytes 1048592 | tf_op jit(solution)/shard_map/reduce_scatter | solution.py:110
  (49 shorter events, 6.6 us)
Async XLA Ops:
  7.2 38.3 %copy-start = (bf16[512,1024]{1,0:T(8,128)(2,1)S(1)}, bf16[512,1024]{1,0:T(8,128)(2,1)}, u32[]{:S(2)}) copy-start(bf16[512,1024]{1,0:T(8,128)(2,1)} %param.8) | copy-start | bytes 3145732
  7.2 25.0 %all-gather.6.cloned.1.call-start = ((), (), s32[]{:S(2)}) async-start(), calls=%async_computation.2 | async-start | bytes 12582912 | tf_op jit(solution)/shard_map/all_gather | solution.py:47
  7.9 33.4 %copy-start.9 = (bf16[512,1024]{1,0:T(8,128)(2,1)S(1)}, bf16[512,1024]{1,0:T(8,128)(2,1)}, u32[]{:S(2)}) copy-start(bf16[512,1024]{1,0:T(8,128)(2,1)} %param.9) | copy-start | bytes 3145732
  7.9 63.9 %all-gather.8.cloned.1.call-start = ((), (), s32[]{:S(2)}) async-start(), calls=%async_computation.5 | async-start | bytes 2359296 | tf_op jit(solution)/shard_map/all_gather | solution.py:12
  41.3 5.5 %copy-start.6 = (bf16[64,8,8,128]{3,2,1,0:T(8,128)(2,1)}, bf16[64,8,8,128]{3,2,1,0:T(8,128)(2,1)S(1)}, u32[]{:S(2)}) copy-start(bf16[64,8,8,128]{3,2,1,0:T(8,128)(2,1)S(1)} %fusion.2) | copy-start | bytes 3145732
  42.7 70.9 %all-gather.10.cloned.1.call-start = ((), (), s32[]{:S(2)}) async-start(), calls=%async_computation.6 | async-start | bytes 2359296 | tf_op jit(solution)/shard_map/all_gather | solution.py:72
  45.5 1.3 copy-start.12
  46.8 2.0 copy-start.5
  71.9 3.0 %copy-start.2 = (f32[8,128,128]{2,1,0:T(8,128)}, f32[8,128,128]{2,1,0:T(8,128)S(1)}, u32[]{:S(2)}) copy-start(f32[8,128,128]{2,1,0:T(8,128)S(1)} %get-tuple-element.27) | copy-start | bytes 1572868
  71.9 3.1 %copy-start.4 = (f32[512,1024]{0,1:T(8,128)S(1)}, f32[512,1024]{0,1:T(8,128)}, u32[]{:S(2)}) copy-start(f32[512,1024]{0,1:T(8,128)} %copy.60) | copy-start | bytes 6291460
  78.2 118.8 %reduce-scatter.5.cloned.1.call-start = ((), (), s32[]{:S(2)}) async-start(), calls=%async_computation.4 | async-start | bytes 9437184 | tf_op jit(solution)/shard_map/reduce_scatter | solution.py:93
  113.6 2.2 copy-start.8
  115.8 2.9 %copy-start.13 = (bf16[512,4096]{1,0:T(8,128)(2,1)S(1)}, bf16[512,4096]{1,0:T(8,128)(2,1)}, u32[]{:S(2)}) copy-start(bf16[512,4096]{1,0:T(8,128)(2,1)} %param.7) | copy-start | bytes 12582916
  117.8 1.0 copy-start.11
  125.5 151.0 %reduce-scatter.3.cloned.1.call-start = ((), (), s32[]{:S(2)}) async-start(), calls=%async_computation.3 | async-start | bytes 5242880 | tf_op jit(solution)/shard_map/reduce_scatter | solution.py:110
  136.2 3.0 %copy-start.10 = (bf16[512,1024]{1,0:T(8,128)(2,1)S(1)}, bf16[512,1024]{1,0:T(8,128)(2,1)}, u32[]{:S(2)}) copy-start(bf16[512,1024]{1,0:T(8,128)(2,1)} %param.9) | copy-start | bytes 3145732
  139.2 2.0 copy-start.1
  139.2 2.0 copy-start.3
  146.5 3.1 %copy-start.7 = (bf16[64,8,8,128]{3,2,1,0:T(8,128)(2,1)S(1)}, bf16[64,8,8,128]{3,2,1,0:T(8,128)(2,1)}, u32[]{:S(2)}) copy-start(bf16[64,8,8,128]{3,2,1,0:T(8,128)(2,1)} %copy-done.6) | copy-start | bytes 3145732
Sparse Core Ops, SparseCore 0:
  9.5 22.5 all-gather.5
  42.9 28.9 all-gather.7
  78.3 35.2 all-gather.9
  125.6 71.2 reduce-scatter.4
  199.7 76.7 reduce-scatter.2
where the time goes:
time: 283 us
  waiting for transfers between devices  199 us (70%)
  matrix products  52.6 us (19%)
  between operations  14.1 us (5%)
  local copies, waits for them, and re-layouts  13.9 us (5%)
  other arithmetic  3.41 us (1%)
    reduce_scatter x1, waiting for transfers between devices, local(): lax.psum_scatter(partial_input.astype(jnp.bfloat16), 'head', scatter_dime...  77 us
    reduce_scatter x1, waiting for transfers between devices, local(): lax.psum_scatter((lax.dot_general(layer_input, value_grad, (((0,), (0,)),...  45.6 us
    all_gather x1, waiting for transfers between devices, local(): lax.all_gather(as_sent(local_grad[None]), ('ctx', 'fsdp'), axis=0, tiled=...  31 us
    all_gather x1, waiting for transfers between devices, local(): weight_full = lax.all_gather(value_weight, 'fsdp', axis=0, tiled=True)  24.2 us
    all_gather x1, waiting for transfers between devices, entering(): gathered = lax.all_gather(array.astype(jnp.bfloat16), axis)  20.2 us
    dot_general x7, matrix products, lowdot(): jnp.einsum(pattern, former, latter, preferred_element_type=jnp.float32)  16.5 us
    dot_general x1, matrix products, local(): lax.dot_general(value_grad, weight_full, (((1,), (1,)), ((), ())), prefer...  10.6 us
    unnamed x31, local copies, waits for them, and re-layouts  9.62 us
  transfers between devices with their start and end apart: 5, of which 5 were waited for; matrix products, arithmetic and copies ran while one was open for 14% of the time, Pallas kernels for 0%

commit v1 on v0

--- a/solution.py
+++ b/solution.py
@@ -44,7 +44,9 @@
 
 def local(layer_input, query_act, key_act, out_grad, value_weight):
     tok_rows = layer_input.shape[0]
-    weight_full = lax.all_gather(value_weight, "fsdp", axis=0, tiled=True)
+    weight_full = jnp.concatenate(
+        lax.all_to_all(jnp.stack([value_weight] * lax.axis_size("fsdp")), "fsdp", 0, 0), axis=0
+    )
     value_act = jnp.dot(layer_input, weight_full, preferred_element_type=jnp.float32).astype(
         jnp.bfloat16
     )

time: 283 us -> 275 us (0.972)
  waiting for transfers between devices: 199 us -> 176 us
  blocking collectives: 0 us -> 12.3 us
  other arithmetic: 3.41 us -> 10.9 us
  matrix products: 52.6 us -> 47.7 us
    all_gather x1 -> x0, waiting for transfers between devices: 24.2 us -> none  [local(): weight_full = lax.all_gather(value_weight, 'fsdp', axis=0, tiled=True)]
    all_to_all x0 -> x1, blocking collectives: none -> 12.3 us  [local(): lax.all_to_all(jnp.stack([value_weight] * lax.axis_size('fsdp')), 'fsdp',...]
    another operation x0 -> x1, other arithmetic: none -> 7.51 us  [local(): jnp.stack([value_weight] * lax.axis_size('fsdp'))]
    dot_general x1, matrix products: 9.14 us -> 4.54 us  [local(): jnp.dot(layer_input, weight_full, preferred_element_type=jnp.float32)]
    unnamed x31 -> x35, local copies, waits for them, and re-layouts: 9.62 us -> 9.56 us
  transfers between devices with their start and end apart: 5 -> 4, of which waited for: 5 -> 4; matrix products, arithmetic and copies ran while one was open for 14% -> 14% of each run, Pallas kernels for 0% -> 0%
where the time goes in v1:
time: 275 us
  waiting for transfers between devices  176 us (64%)
  matrix products  47.7 us (17%)
  between operations  14.1 us (5%)
  local copies, waits for them, and re-layouts  13.8 us (5%)
  blocking collectives  12.3 us (4%)
  other arithmetic  10.9 us (4%)
    reduce_scatter x1, waiting for transfers between devices, local(): lax.psum_scatter(partial_input.astype(jnp.bfloat16), 'head', scatter_dime...  77 us
    reduce_scatter x1, waiting for transfers between devices, local(): lax.psum_scatter((lax.dot_general(layer_input, value_grad, (((0,), (0,)),...  45.5 us
    all_gather x1, waiting for transfers between devices, local(): lax.all_gather(as_sent(local_grad[None]), ('ctx', 'fsdp'), axis=0, tiled=...  31.2 us
    all_gather x1, waiting for transfers between devices, entering(): gathered = lax.all_gather(array.astype(jnp.bfloat16), axis)  21.8 us
    dot_general x7, matrix products, lowdot(): jnp.einsum(pattern, former, latter, preferred_element_type=jnp.float32)  16.3 us
    all_to_all x1, blocking collectives, local(): lax.all_to_all(jnp.stack([value_weight] * lax.axis_size('fsdp')), 'fsdp',...  12.3 us
    dot_general x1, matrix products, local(): lax.dot_general(value_grad, weight_full, (((1,), (1,)), ((), ())), prefer...  10.6 us
    dot_general x5, matrix products, product(): return jnp.einsum(pattern, former, latter, precision=lax.Precision.HIGHEST)  9.56 us
  transfers between devices with their start and end apart: 4, of which 4 were waited for; matrix products, arithmetic and copies ran while one was open for 14% of the time, Pallas kernels for 0%

profile of v1, /device:TPU:0, one launch (start us, length us, event | category | flops | bytes accessed | tf_op | source)
XLA Modules:
  0.0 275.0 jit_solution(5808316055956517193)
XLA Ops:
  7.2 7.5 %pad_maximum_fusion = bf16[2,2048,1024]{2,1,0:T(8,128)(2,1)} fusion(bf16[1,2048,1024]{2,1,0:T(8,128)(2,1)} %bitcast.111), kind=kLoop, calls=%fused_computation.2 | loop fusion | flops 4194304 | bytes 12582912 | tf_op jit(solution)/shard_map/stack | solution.py:48
  14.7 12.3 %all_to_all.5 = bf16[2,2048,1024]{2,1,0:T(8,128)(2,1)S(1)} all-to-all(bf16[2,2048,1024]{2,1,0:T(8,128)(2,1)} %pad_maximum_fusion), channel_id=1, replica_groups=mesh['ctx'=4,'head'=4,'fsdp'=2] {'fsdp'}, dimensions={0} | all-to-all | bytes 16777216 | tf_op jit(solution)/shard_map/all_to_all | solution.py:48
  27.1 4.5 %convolution_convert_fusion.1 = bf16[1024,512]{1,0:T(8,128)(2,1)S(1)} fusion(bf16[4096,1024]{1,0:T(8,128)(2,1)S(1)} %bitcast.109, bf16[512,4096]{1,0:T(8,128)(2,1)S(1)} %copy-done.14), kind=kOutput, calls=%fused_computation.17 | convolution fusion | flops 4295491584 | bytes 13631488 | tf_op jit(solution)/shard_map/dot_general | solution.py:50
  33.1 2.6 copy.54
  35.7 1.3 select_convert_fusion.1
  37.1 2.0 copy-done.5
  39.0 2.8 %fusion.25 = f32[8,128,512]{2,1,0:T(8,128)} fusion(bf16[512,8,128]{0,2,1:T(8,128)(2,1)S(1)} %bitcast.106, bf16[8,512,512]{2,1,0:T(8,128)(2,1)S(1)} %select_convert_fusion.1), kind=kOutput, calls=%fused_computation.47 | convolution fusion | flops 536870912 | bytes 7340032 | tf_op jit(solution)/shard_map/hts,shj->thj/dot_general | solution.py:30
  41.8 21.8 %all-gather.5.cloned.1.call-done = bf16[64,128,128]{2,1,0:T(8,128)(2,1)} async-done(((bf16[8,128,128]{2,1,0:T(8,128)(2,1)}), bf16[64,128,128]{2,1,0:T(8,128)(2,1)}) %all-gather.5.cloned.1.call-update) | async-done | bytes 2097168 | tf_op jit(solution)/shard_map/all_gather | solution.py:12
  63.9 3.0 %fusion.1 = (f32[512,8]{0,1:T(8,128)S(1)}, f32[8,128,512]{2,1,0:T(8,128)S(1)}) fusion(f32[8,128,512]{2,1,0:T(8,128)} %fusion.25, f32[8,128,128]{2,1,0:T(8,128)S(1)} %get-tuple-element.27, bf16[512,1024]{1,0:T(8,128)(2,1)S(1)} %copy-done), kind=kOutput, calls=%fused_computation.9 | convolution fusion | flops 806875136 | bytes 5783552 | tf_op jit(solution)/shard_map/thi,hij->thj/dot_general | solution.py:26
  70.2 4.2 %fusion.22 = f32[8,128,512]{2,1,0:T(8,128)} fusion(bf16[8,512,512]{2,1,0:T(8,128)(2,1)} %copy-done.5, f32[512,8,128]{0,2,1:T(8,128)S(1)} %subtract_multiply_fusion), kind=kOutput, calls=%fused_computation.41 | convolution fusion | flops 537395200 | bytes 8388608 | tf_op jit(solution)/shard_map/hts,thj->shj/dot_general | solution.py:30
  74.4 31.2 %all-gather.7.cloned.1.call-done = bf16[64,128,128]{2,1,0:T(8,128)(2,1)} async-done(((bf16[8,128,128]{2,1,0:T(8,128)(2,1)}), bf16[64,128,128]{2,1,0:T(8,128)(2,1)}) %all-gather.7.cloned.1.call-update) | async-done | bytes 2097168 | tf_op jit(solution)/shard_map/all_gather | solution.py:74
  105.6 2.2 select_reduce_fusion
  107.9 1.9 add_convert_fusion
  110.7 6.7 %fusion = bf16[4096,1024]{0,1:T(8,128)(2,1)} fusion(bf16[512,1024]{0,1:T(8,128)(2,1)S(1)} %bitcast.115, bf16[512,4096]{1,0:T(8,128)(2,1)S(1)} %copy-done.15), kind=kOutput, calls=%fused_computation.5 | convolution fusion | flops 4303355904 | bytes 13631488 | tf_op jit(solution)/shard_map/dot_general | solution.py:97
  117.7 10.6 %convolution_convert_fusion = bf16[512,4096]{1,0:T(8,128)(2,1)} fusion(bf16[512,1024]{0,1:T(8,128)(2,1)} %bitcast.116, bf16[4096,1024]{1,0:T(8,128)(2,1)} %bitcast.110), kind=kOutput, calls=%fused_computation.6 | convolution fusion | flops 4297064448 | bytes 13631488 | tf_op jit(solution)/shard_map/dot_general | solution.py:109
  128.3 3.0 %select_convert_fusion = bf16[8,512,512]{2,1,0:T(8,128)(2,1)S(1)} fusion(pred[512,512]{1,0:T(8,128)(4,1)} %copy-done.13, bf16[512,8,128]{0,2,1:T(8,128)(2,1)} %bitcast.107, f32[512,8,128]{0,2,1:T(8,128)S(1)} %subtract_multiply_fusion), kind=kOutput, calls=%fused_computation.3 | convolution fusion | flops 541589504 | bytes 7602176 | tf_op jit(solution)/shard_map/thj,shj->hts/dot_general | solution.py:30
  131.3 1.5 fusion.4
  133.2 3.0 %add_convert_fusion.2 = bf16[8,512,128]{1,2,0:T(8,128)(2,1)} fusion(f32[8,512,128]{1,2,0:T(8,128)S(1)} %fusion.4, f32[512,8,128]{0,2,1:T(8,128)S(1)} %subtract_multiply_fusion, f32[8,128,128]{2,1,0:T(8,128)S(1)} %copy-done.3), kind=kOutput, calls=%fused_computation.13 | convolution fusion | flops 806354944 | bytes 5767168 | tf_op jit(solution)/shard_map/hij,thj->thi/dot_general | solution.py:26
  136.3 2.3 copy.65
  138.6 3.1 %fusion.9 = f32[8,512,128]{1,2,0:T(8,128)S(1)} fusion(bf16[8,512,512]{2,1,0:T(8,128)(2,1)} %copy-done.1, bf16[512,1024]{1,0:T(8,128)(2,1)S(1)} %copy-done), kind=kOutput, calls=%fused_computation.27 | convolution fusion | flops 536870912 | bytes 7340032 | tf_op jit(solution)/shard_map/hts,thi->shi/dot_general | solution.py:30
  142.1 1.3 copy.66
  143.4 45.5 %reduce-scatter.5.cloned.1.call-done = bf16[512,1024]{0,1:T(8,128)(2,1)} async-done(((bf16[4096,1024]{0,1:T(8,128)(2,1)}), bf16[512,1024]{0,1:T(8,128)(2,1)}) %reduce-scatter.5.cloned.1.call-update) | async-done | bytes 1048592 | tf_op jit(solution)/shard_map/reduce_scatter | solution.py:95
  188.9 2.6 copy.67
  191.5 77.0 %reduce-scatter.3.cloned.1.call-done = bf16[512,1024]{1,0:T(8,128)(2,1)} async-done(((bf16[512,4096]{1,0:T(8,128)(2,1)}), bf16[512,1024]{1,0:T(8,128)(2,1)}) %reduce-scatter.3.cloned.1.call-update) | async-done | bytes 1048592 | tf_op jit(solution)/shard_map/reduce_scatter | solution.py:112
  (52 shorter events, 7.1 us)
Async XLA Ops:
  7.2 28.5 %copy-start = (bf16[512,1024]{1,0:T(8,128)(2,1)S(1)}, bf16[512,1024]{1,0:T(8,128)(2,1)}, u32[]{:S(2)}) copy-start(bf16[512,1024]{1,0:T(8,128)(2,1)} %param.8) | copy-start | bytes 3145732
  7.2 56.5 %all-gather.5.cloned.1.call-start = ((), (), s32[]{:S(2)}) async-start(), calls=%async_computation.5 | async-start | bytes 2359296 | tf_op jit(solution)/shard_map/all_gather | solution.py:12
  14.7 12.3 %copy-start.14 = (bf16[512,4096]{1,0:T(8,128)(2,1)S(1)}, bf16[512,4096]{1,0:T(8,128)(2,1)}, u32[]{:S(2)}) copy-start(bf16[512,4096]{1,0:T(8,128)(2,1)} %param.7) | copy-start | bytes 12582916
  27.1 4.6 %copy-start.8 = (bf16[2,2048,1024]{2,1,0:T(8,128)(2,1)}, bf16[2,2048,1024]{2,1,0:T(8,128)(2,1)S(1)}, u32[]{:S(2)}) copy-start(bf16[2,2048,1024]{2,1,0:T(8,128)(2,1)S(1)} %all_to_all.5) | copy-start | bytes 25165828
  27.1 4.6 %copy-start.10 = (bf16[512,1024]{1,0:T(8,128)(2,1)S(1)}, bf16[512,1024]{1,0:T(8,128)(2,1)}, u32[]{:S(2)}) copy-start(bf16[512,1024]{1,0:T(8,128)(2,1)} %param.9) | copy-start | bytes 3145732
  31.6 5.4 %copy-start.6 = (bf16[1024,512]{1,0:T(8,128)(2,1)}, bf16[1024,512]{1,0:T(8,128)(2,1)S(1)}, u32[]{:S(2)}) copy-start(bf16[1024,512]{1,0:T(8,128)(2,1)S(1)} %convolution_convert_fusion.1) | copy-start | bytes 3145732
  33.0 72.6 %all-gather.7.cloned.1.call-start = ((), (), s32[]{:S(2)}) async-start(), calls=%async_computation.6 | async-start | bytes 2359296 | tf_op jit(solution)/shard_map/all_gather | solution.py:74
  35.7 1.3 copy-start.13
  37.1 2.0 copy-start.5
  63.9 3.0 %copy-start.2 = (f32[8,128,128]{2,1,0:T(8,128)}, f32[8,128,128]{2,1,0:T(8,128)S(1)}, u32[]{:S(2)}) copy-start(f32[8,128,128]{2,1,0:T(8,128)S(1)} %get-tuple-element.27) | copy-start | bytes 1572868
  63.9 3.1 %copy-start.4 = (f32[512,1024]{0,1:T(8,128)S(1)}, f32[512,1024]{0,1:T(8,128)}, u32[]{:S(2)}) copy-start(f32[512,1024]{0,1:T(8,128)} %copy.54) | copy-start | bytes 6291460
  70.1 118.8 %reduce-scatter.5.cloned.1.call-start = ((), (), s32[]{:S(2)}) async-start(), calls=%async_computation.4 | async-start | bytes 9437184 | tf_op jit(solution)/shard_map/reduce_scatter | solution.py:95
  105.6 2.2 copy-start.9
  107.8 2.9 %copy-start.15 = (bf16[512,4096]{1,0:T(8,128)(2,1)S(1)}, bf16[512,4096]{1,0:T(8,128)(2,1)}, u32[]{:S(2)}) copy-start(bf16[512,4096]{1,0:T(8,128)(2,1)} %param.7) | copy-start | bytes 12582916
  109.8 1.0 copy-start.12
  117.4 151.0 %reduce-scatter.3.cloned.1.call-start = ((), (), s32[]{:S(2)}) async-start(), calls=%async_computation.3 | async-start | bytes 5242880 | tf_op jit(solution)/shard_map/reduce_scatter | solution.py:112
  128.3 3.0 %copy-start.11 = (bf16[512,1024]{1,0:T(8,128)(2,1)S(1)}, bf16[512,1024]{1,0:T(8,128)(2,1)}, u32[]{:S(2)}) copy-start(bf16[512,1024]{1,0:T(8,128)(2,1)} %param.9) | copy-start | bytes 3145732
  131.3 2.0 copy-start.1
  131.3 1.9 copy-start.3
  138.6 3.1 %copy-start.7 = (bf16[1024,512]{1,0:T(8,128)(2,1)S(1)}, bf16[1024,512]{1,0:T(8,128)(2,1)}, u32[]{:S(2)}) copy-start(bf16[1024,512]{1,0:T(8,128)(2,1)} %copy-done.6) | copy-start | bytes 3145732
Sparse Core Ops, SparseCore 0:
  33.1 30.4 all-gather.4
  70.3 35.2 all-gather.6
  117.6 71.3 reduce-scatter.4
  191.6 76.7 reduce-scatter.2
